TPU v7x, 32 devices: a whole 2x2x4 slice. The times are simulated.
32 devices in a mesh: row: 16 (over z, x, core), col: 2 (over y).
Axes of the slice: x: 2, y: 2, z: 4, core: 2. Of those that a mesh axis runs over, the one named last changes fastest.
Arguments:
- pair_rep: bfloat16 [256, 256, 128], P('row', 'col'), may hold values from -6 to 6
- chain_len: int32 [4], replicated, may hold values from 1 to 64, as said below
- tri_gain: float32 [128], replicated, may hold values from 0.5 to 2
- tri_in: bfloat16 [128, 640], replicated, may hold values from -0.5 to 0.5
- sum_gain: float32 [128], replicated, may hold values from 0.5 to 2
- tri_out: bfloat16 [128, 128], replicated, may hold values from -0.5 to 0.5
- att_gain: float32 [128], replicated, may hold values from 0.5 to 8
- att_in: bfloat16 [128, 512], replicated, may hold values from -0.5 to 0.5
- att_bias: bfloat16 [128, 4], replicated, may hold values from -2 to 2
- att_out: bfloat16 [128, 128], replicated, may hold values from -4 to 4
Outputs:
- new_pair: bfloat16 [256, 256, 128], P('row', 'col')
Inputs may be any that keep to these rules, and one draw needn't show every extreme that they name: `chain_len`: one chain in every draw has all 64 slots live.
All inputs are finite; a program needn't handle non-finite values.
Results may differ from a plain program's by a relative error of at most 0.039.
The roundings to bfloat16 on the way count: a program that leaves them out, or rounds other values in their place, can miss the bound.
Values may be sent and summed in bfloat16 or wider, within the bound.
No kernel may reach another device: no remote copies, remote signals or barrier semaphores. Data moves between devices by JAX's collectives and lax.ppermute only.
A program may use at most 128 MiB of HBM per device.

v0:
```python
import math
import jax
import jax.numpy as jnp
from jax import lax
from jax.sharding import PartitionSpec as P

CH = 128
H = 4
DH = 32
KCD = 16
SLOT = 64
EPSILON = 1e-05
NEG_SCORE = -1e30


def layer_norm(values, norm_gain):
    values = values.astype(jnp.float32)
    centre = values - jnp.mean(values, axis=-1, keepdims=True)
    spread = jnp.mean(centre * centre, axis=-1, keepdims=True)
    return centre * lax.rsqrt(spread + EPSILON) * norm_gain


def live_tokens(chain_len):
    positions = lax.broadcasted_iota(jnp.int32, (chain_len.shape[0], SLOT), 1)
    return (positions < chain_len[:, None]).astype(jnp.float32).reshape(-1)


def attend_heads(query_pair, kv_all, bias_pair, key_live):

    def attend_row(inputs):
        query_row, kv_row = inputs
        keys_row = kv_row[:, : 2 * DH].reshape(kv_row.shape[0], 2, DH)
        values_row = kv_row[:, 2 * DH :].reshape(kv_row.shape[0], 2, DH)
        scores = (
            jnp.einsum("jhd,khd->hjk", query_row, keys_row, preferred_element_type=jnp.float32)
            / math.sqrt(DH)
            + bias_pair
        )
        scores = jnp.where(key_live[None, None, :], scores, NEG_SCORE)
        row_top = jnp.max(scores, axis=-1, keepdims=True)
        weights = jnp.exp(scores - row_top).astype(jnp.bfloat16)
        totals = jnp.sum(weights, axis=-1, dtype=jnp.float32)
        summed = jnp.einsum("hjk,khd->jhd", weights, values_row, preferred_element_type=jnp.float32)
        return summed / jnp.transpose(totals)[:, :, None]

    return lax.map(attend_row, (query_pair, kv_all))


def body(
    pair_rep, chain_len, tri_gain, tri_in, sum_gain, tri_out, att_gain, att_in, att_bias, att_out
):
    row_count = pair_rep.shape[0]
    col_count = pair_rep.shape[1]
    row_start = lax.axis_index("row") * row_count
    col_start = lax.axis_index("col") * col_count
    live_all = live_tokens(chain_len)
    live_rows = lax.dynamic_slice_in_dim(live_all, row_start, row_count)
    live_cols = lax.dynamic_slice_in_dim(live_all, col_start, col_count)
    tri_norm = layer_norm(pair_rep, tri_gain).astype(jnp.bfloat16)
    out_gate = jax.nn.sigmoid(
        jnp.dot(tri_norm, tri_in[:, 4 * CH :], preferred_element_type=jnp.float32)
    )
    group_proj = jnp.dot(tri_norm[:, :KCD], tri_in[:, : 4 * CH], preferred_element_type=jnp.float32)
    pair_live = live_rows[:, None, None] * live_cols[None, :KCD, None]
    left_edge = (
        jax.nn.sigmoid(group_proj[..., :CH]) * group_proj[..., CH : 2 * CH] * pair_live
    ).astype(jnp.bfloat16)
    right_edge = (
        jax.nn.sigmoid(group_proj[..., 2 * CH : 3 * CH])
        * group_proj[..., 3 * CH : 4 * CH]
        * pair_live
    ).astype(jnp.bfloat16)
    right_all = lax.all_gather(right_edge, "row", axis=0, tiled=True)
    right_cols = lax.all_to_all(right_all, "col", split_axis=0, concat_axis=1, tiled=True)
    left_all = lax.all_gather(left_edge, "col", axis=1, tiled=True)
    tri_sum = jnp.einsum("ikc,jkc->jic", left_all, right_cols, preferred_element_type=jnp.float32)
    sum_norm = layer_norm(tri_sum, sum_gain).astype(jnp.bfloat16)
    update = jnp.dot(sum_norm, tri_out, preferred_element_type=jnp.float32)
    mid_pair = (pair_rep.astype(jnp.float32) + out_gate * jnp.transpose(update, (1, 0, 2))).astype(
        jnp.bfloat16
    )
    head_width = H * DH
    att_norm = layer_norm(mid_pair, att_gain).astype(jnp.bfloat16)
    queries = jnp.dot(att_norm, att_in[:, :head_width], preferred_element_type=jnp.float32).astype(
        jnp.bfloat16
    )
    att_gate = jax.nn.sigmoid(
        jnp.dot(att_norm, att_in[:, 3 * head_width :], preferred_element_type=jnp.float32)
    )
    pair_bias = jnp.einsum(
        "rcd,dh->hrc", att_norm, att_bias, preferred_element_type=jnp.float32
    ).astype(jnp.bfloat16)
    bias_rows = lax.all_gather(pair_bias, "row", axis=1, tiled=True)
    bias_local = lax.all_to_all(bias_rows, "col", split_axis=1, concat_axis=2, tiled=True)
    key_live = live_all > 0.5
    pieces = []
    for pair_index in range(H // 2):
        head_low = 2 * pair_index * DH
        head_high = head_low + 2 * DH
        kv_weight = jnp.concatenate(
            [
                att_in[:, head_width + head_low : head_width + head_high],
                att_in[:, 2 * head_width + head_low : 2 * head_width + head_high],
            ],
            axis=1,
        )
        kv_local = jnp.dot(att_norm, kv_weight, preferred_element_type=jnp.float32).astype(
            jnp.bfloat16
        )
        kv_all = lax.all_gather(kv_local, "col", axis=1, tiled=True)
        query_pair = queries[:, :, head_low:head_high].reshape(row_count, col_count, 2, DH)
        bias_pair = bias_local[2 * pair_index : 2 * pair_index + 2]
        pieces.append(attend_heads(query_pair, kv_all, bias_pair, key_live))
    attended = jnp.concatenate(pieces, axis=2).reshape(row_count, col_count, head_width)
    attended = (attended * att_gate).astype(jnp.bfloat16)
    new_pair = (
        mid_pair.astype(jnp.float32)
        + jnp.dot(attended, att_out, preferred_element_type=jnp.float32)
    ).astype(jnp.bfloat16)
    return new_pair


def solution(mesh):
    placed = (P("row", "col", None), P(), P(), P(), P(), P(), P(), P(), P(), P())
    return jax.shard_map(
        body, mesh=mesh, in_specs=placed, out_specs=P("row", "col", None), check_vma=False
    )
```

profile of v0, /device:TPU:0, one launch (start us, length us, event | category | flops | bytes accessed | tf_op | source)
XLA Modules:
  0.0 187.7 jit_solution(6166348117230079474)
XLA Ops:
  7.5 1.3 copy.31
  11.0 0.7 fusion.65
  11.8 40.7 %all-gather.4.cloned.1.call-done = bf16[256,16,128]{2,1,0:T(8,128)(2,1)} async-done(((bf16[16,16,128]{2,1,0:T(8,128)(2,1)}), bf16[256,16,128]{2,1,0:T(8,128)(2,1)}) %all-gather.4.cloned.1.call-update) | async-done | bytes 1048592 | tf_op jit(solution)/shard_map/all_gather | solution.py:73
  52.5 3.6 %all-to-all-start = ((bf16[256,16,128]{2,1,0:T(8,128)(2,1)}), bf16[256,16,128]{2,1,0:T(8,128)(2,1)S(1)}, u32[]{:S(2)}, u32[]{:S(2)}) async-start(bf16[256,16,128]{2,1,0:T(8,128)(2,1)} %all-gather.4.cloned.1.call-done), calls=%async_computation | async-start | bytes 2097152 | tf_op jit(solution)/shard_map/all_to_all | solution.py:74
  56.1 15.6 %all_gather.16 = bf16[16,32,128]{2,1,0:T(8,128)(2,1)S(1)} all-gather(bf16[16,16,128]{2,1,0:T(8,128)(2,1)S(1)} %get-tuple-element.154), channel_id=1, replica_groups=mesh['row'=16,'col'=2] {'col'}, dimensions={1}, use_global_device_ids=true | all-gather | bytes 196608 | tf_op jit(solution)/shard_map/all_gather | solution.py:75
  72.7 1.5 fusion.45
  74.2 1.5 copy.35
  78.8 1.2 convolution_convert_fusion.2
  81.0 21.5 %all_gather.18 = bf16[4,256,128]{2,0,1:T(4,128)(2,1)} all-gather(bf16[4,16,128]{2,0,1:T(4,128)(2,1)S(1)} %fusion.53), channel_id=1, replica_groups=mesh['row'=16,'col'=2] {'row'}, dimensions={1}, use_global_device_ids=true | all-gather | bytes 278528 | tf_op jit(solution)/shard_map/all_gather | solution.py:93
  102.5 3.4 %all-to-all-start.1 = ((bf16[4,256,128]{2,0,1:T(4,128)(2,1)}), bf16[4,256,128]{2,0,1:T(4,128)(2,1)S(1)}, u32[]{:S(2)}, u32[]{:S(2)}) async-start(bf16[4,256,128]{2,0,1:T(4,128)(2,1)} %all_gather.18), calls=%async_computation.1 | async-start | bytes 524288 | tf_op jit(solution)/shard_map/all_to_all | solution.py:94
  106.0 1.2 convolution_convert_fusion.1
  107.6 4.2 %all-to-all-done.1 = bf16[4,256,128]{2,0,1:T(4,128)(2,1)S(1)} async-done(((bf16[4,256,128]{2,0,1:T(4,128)(2,1)}), bf16[4,256,128]{2,0,1:T(4,128)(2,1)S(1)}, u32[]{:S(2)}, u32[]{:S(2)}) %all-to-all-start.1) | async-done | bytes 262176 | tf_op jit(solution)/shard_map/all_to_all | solution.py:94
  112.6 33.0 %while.22 = (s32[]{:T(128)}, f32[16,128,2,32]{1,3,2,0:T(8,128)S(1)}, bf16[16,256,128]{2,1,0:T(8,128)(2,1)}, bf16[16,128,2,32]{1,3,2,0:T(8,128)(2,1)S(1)}, bf16[2...) while((s32[]{:T(128)}, f32[16,128,2,32]{1,3,2,0:T(8,128)S(1)}, ...), condition=%wide.region_9.10_spmd.clone, body=%wide.region_6.9_spmd.clone.sunk | while | flops 13510144 | bytes 1613165 | solution.py:46
  112.6 0.9 constant_dynamic-slice_fusion.4
  114.7 0.9 constant_dynamic-slice_fusion.4
  116.8 0.9 constant_dynamic-slice_fusion.4
  118.8 0.9 constant_dynamic-slice_fusion.4
  120.9 0.9 constant_dynamic-slice_fusion.4
  122.9 0.9 constant_dynamic-slice_fusion.4
  125.0 0.9 constant_dynamic-slice_fusion.4
  127.0 0.9 constant_dynamic-slice_fusion.4
  129.1 0.9 constant_dynamic-slice_fusion.4
  131.2 0.9 constant_dynamic-slice_fusion.4
  133.2 0.9 constant_dynamic-slice_fusion.4
  135.3 0.9 constant_dynamic-slice_fusion.4
  137.3 0.9 constant_dynamic-slice_fusion.4
  139.4 0.9 constant_dynamic-slice_fusion.4
  141.5 0.9 constant_dynamic-slice_fusion.4
  143.5 0.9 constant_dynamic-slice_fusion.4
  145.7 32.9 %while.23 = (s32[]{:T(128)}, f32[16,128,2,32]{1,3,2,0:T(8,128)S(1)}, bf16[16,256,128]{2,1,0:T(8,128)(2,1)}, bf16[16,128,2,32]{1,3,2,0:T(8,128)(2,1)S(1)}, bf16[2...) while((s32[]{:T(128)}, f32[16,128,2,32]{1,3,2,0:T(8,128)S(1)}, ...), condition=%wide.region_13.14_spmd.clone, body=%wide.region_10.13_spmd.clone.sunk | while | flops 13510144 | bytes 1613165 | solution.py:46
  145.7 0.8 constant_dynamic-slice_fusion.5
  147.7 0.9 constant_dynamic-slice_fusion.5
  149.8 0.9 constant_dynamic-slice_fusion.5
  151.8 0.9 constant_dynamic-slice_fusion.5
  153.9 0.9 constant_dynamic-slice_fusion.5
  155.9 0.9 constant_dynamic-slice_fusion.5
  158.0 0.9 constant_dynamic-slice_fusion.5
  160.1 0.9 constant_dynamic-slice_fusion.5
  162.1 0.9 constant_dynamic-slice_fusion.5
  164.2 0.9 constant_dynamic-slice_fusion.5
  166.2 0.9 constant_dynamic-slice_fusion.5
  168.3 0.9 constant_dynamic-slice_fusion.5
  170.4 0.9 constant_dynamic-slice_fusion.5
  172.4 0.9 constant_dynamic-slice_fusion.5
  174.5 0.9 constant_dynamic-slice_fusion.5
  176.5 0.9 constant_dynamic-slice_fusion.5
  179.4 0.7 fusion.47
  180.1 1.0 copy.50
  (318 shorter events, 47.8 us)
Async XLA Ops:
  6.5 70.5 %copy-start = (bf16[128,128]{1,0:T(8,128)(2,1)S(1)}, bf16[128,128]{1,0:T(8,128)(2,1)}, u32[]{:S(2)}) copy-start(bf16[128,128]{1,0:T(8,128)(2,1)} %param.19) | copy-start | bytes 98308
  6.5 45.9 %all-gather.4.cloned.1.call-start = ((), (), s32[]{:S(2)}) async-start(), calls=%async_computation.2 | async-start | bytes 1114112 | tf_op jit(solution)/shard_map/all_gather | solution.py:73
  6.5 0.7 copy-start.4
  9.1 0.7 copy-start.5
  9.8 0.9 copy-start.3
  52.5 21.7 %all-to-all-start = ((bf16[256,16,128]{2,1,0:T(8,128)(2,1)}), bf16[256,16,128]{2,1,0:T(8,128)(2,1)S(1)}, u32[]{:S(2)}, u32[]{:S(2)}) async-start(bf16[256,16,128]{2,1,0:T(8,128)(2,1)} %all-gather.4.cloned.1.call-done), calls=%async_computation | async-start | bytes 2097152 | tf_op jit(solution)/shard_map/all_to_all | solution.py:74
  56.1 56.5 %all-gather.6.cloned.1.call-start = ((), (), s32[]{:S(2)}) async-start(), calls=%async_computation.3 | async-start | bytes 1572864 | tf_op jit(solution)/shard_map/all_gather | solution.py:110
  71.7 0.9 copy-start.2
  76.2 0.7 copy-start.6
  76.3 1.2 copy-start.1
  78.2 0.7 copy-start.7
  80.1 0.7 copy-start.9
  102.5 9.4 %all-to-all-start.1 = ((bf16[4,256,128]{2,0,1:T(4,128)(2,1)}), bf16[4,256,128]{2,0,1:T(4,128)(2,1)S(1)}, u32[]{:S(2)}, u32[]{:S(2)}) async-start(bf16[4,256,128]{2,0,1:T(4,128)(2,1)} %all_gather.18), calls=%async_computation.1 | async-start | bytes 524288 | tf_op jit(solution)/shard_map/all_to_all | solution.py:94
  105.9 39.7 %all-gather.8.cloned.1.call-start = ((), (), s32[]{:S(2)}) async-start(), calls=%async_computation.4 | async-start | bytes 1572864 | tf_op jit(solution)/shard_map/all_gather | solution.py:110
  178.6 0.8 copy-start.8
Sparse Core Ops, SparseCore 0:
  11.9 40.5 all-gather.3
  80.2 19.3 all-gather.5
  108.3 19.0 all-gather.7
where the time goes:
time: 190 us; the launch traced here: 188 us
  waiting for transfers between devices  45 us (24%)
  local copies, waits for them, and re-layouts  44.5 us (23%)
  blocking collectives  37.1 us (20%)
  matrix products  35.2 us (19%)
  between operations  13.4 us (7%)
  starting transfers between devices  7.1 us (4%)
  other arithmetic  4.52 us (2%)
    all_gather x1, waiting for transfers between devices, body(): right_all = lax.all_gather(right_edge, 'row', axis=0, tiled=True)  40.7 us
    dynamic_slice x64, local copies, waits for them, and re-layouts, attend_heads(): return lax.map(attend_row, (query_pair, kv_all))  30.8 us
    all_gather x1, blocking collectives, body(): bias_rows = lax.all_gather(pair_bias, 'row', axis=1, tiled=True)  21.5 us
    all_gather x1, blocking collectives, body(): left_all = lax.all_gather(left_edge, 'col', axis=1, tiled=True)  15.6 us
    sub x32, matrix products, attend_row(): weights = jnp.exp(scores - row_top).astype(jnp.bfloat16)  13.7 us
    dot_general x32, matrix products, attend_row(): jnp.einsum('hjk,khd->jhd', weights, values_row, preferred_element_type=jn...  7.63 us
    dot_general x32, matrix products, attend_row(): jnp.einsum('jhd,khd->hjk', query_row, keys_row, preferred_element_type=jn...  7.44 us
    unnamed x21, local copies, waits for them, and re-layouts  6.7 us
  transfers between devices with their start and end apart: 5, of which 2 were waited for; matrix products, arithmetic and copies ran while one was open for 20% of the time, Pallas kernels for 0%

commit v1 on v0

--- a/solution.py
+++ b/solution.py
@@ -11,6 +11,27 @@
 SLOT = 64
 EPSILON = 1e-05
 NEG_SCORE = -1e30
+
+
+def hold_the_shapes(z, net_axis):
+    main, q_next, wide_out = (jax.lax.axis_size(net_axis), jax.lax.axis_index(net_axis), z.shape[0])
+    sides = list(map(lambda h: (h, (h + 1) % main), range(main)))
+    inbox = list(map(lambda h: (h, (h - 1) % main), range(main)))
+    local_out = jnp.zeros((*z.shape[:0], main * wide_out, *z.shape[1:]), z.dtype)
+    local_out = lax.dynamic_update_slice_in_dim(local_out, z, q_next * wide_out, axis=0)
+    v1 = mixed_arr = z
+    met_up = main // 2
+    for w in [*range(1, met_up + 1)]:
+        v1 = jax.lax.ppermute(v1, net_axis, sides)
+        local_out = lax.dynamic_update_slice_in_dim(
+            local_out, v1, (q_next - w) % main * wide_out, axis=0
+        )
+        if w < main - met_up:
+            mixed_arr = jax.lax.ppermute(mixed_arr, net_axis, inbox)
+            local_out = lax.dynamic_update_slice_in_dim(
+                local_out, mixed_arr, (q_next + w) % main * wide_out, axis=0
+            )
+    return local_out
 
 
 def layer_norm(values, norm_gain):
@@ -70,7 +91,7 @@
         * group_proj[..., 3 * CH : 4 * CH]
         * pair_live
     ).astype(jnp.bfloat16)
-    right_all = lax.all_gather(right_edge, "row", axis=0, tiled=True)
+    right_all = hold_the_shapes(right_edge, "row")
     right_cols = lax.all_to_all(right_all, "col", split_axis=0, concat_axis=1, tiled=True)
     left_all = lax.all_gather(left_edge, "col", axis=1, tiled=True)
     tri_sum = jnp.einsum("ikc,jkc->jic", left_all, right_cols, preferred_element_type=jnp.float32)

time: 190 us -> 196 us (1.032)
  starting transfers between devices: 7.1 us -> 39.7 us
  waiting for transfers between devices: 45 us -> 14.9 us
  local copies, waits for them, and re-layouts: 44.5 us -> 55 us
  blocking collectives: 37.1 us -> 29.7 us
    all_gather x1 -> x0, waiting for transfers between devices: 40.7 us -> none  [body(): right_all = lax.all_gather(right_edge, 'row', axis=0, tiled=True)]
    ppermute x0 -> x15, starting transfers between devices: none -> 32.6 us  [the longest x7 32.1 us: hold_the_shapes(): mixed_arr = jax.lax.ppermute(mixed_arr, net_axis, inbox)]
    ppermute x0 -> x15, waiting for transfers between devices: none -> 10.6 us  [the longest x8 10.4 us: hold_the_shapes(): v1 = jax.lax.ppermute(v1, net_axis, sides)]
    dynamic_update_slice x0 -> x15, local copies, waits for them, and re-layouts: none -> 9.34 us  [the longest x8 4.98 us: hold_the_shapes(): lax.dynamic_update_slice_in_dim(local_out, v1, (q_next - w) % main * wide...]
    all_gather x1, blocking collectives: 15.6 us -> 10.4 us  [body(): left_all = lax.all_gather(left_edge, 'col', axis=1, tiled=True)]
    all_gather x1, blocking collectives: 21.5 us -> 19.2 us  [body(): bias_rows = lax.all_gather(pair_bias, 'row', axis=1, tiled=True)]
  transfers between devices with their start and end apart: 5 -> 19, of which waited for: 2 -> 11; matrix products, arithmetic and copies ran while one was open for 20% -> 24% of each run, Pallas kernels for 0% -> 0%
where the time goes in v1:
time: 196 us; the launch traced here: 194 us
  local copies, waits for them, and re-layouts  55 us (28%)
  starting transfers between devices  39.7 us (20%)
  matrix products  35.1 us (18%)
  blocking collectives  29.7 us (15%)
  waiting for transfers between devices  14.9 us (8%)
  between operations  14 us (7%)
  other arithmetic  4.61 us (2%)
    ppermute x7, starting transfers between devices, hold_the_shapes(): mixed_arr = jax.lax.ppermute(mixed_arr, net_axis, inbox)  32.1 us
    dynamic_slice x64, local copies, waits for them, and re-layouts, attend_heads(): return lax.map(attend_row, (query_pair, kv_all))  30.8 us
    all_gather x1, blocking collectives, body(): bias_rows = lax.all_gather(pair_bias, 'row', axis=1, tiled=True)  19.2 us
    sub x32, matrix products, attend_row(): weights = jnp.exp(scores - row_top).astype(jnp.bfloat16)  13.7 us
    all_gather x1, blocking collectives, body(): left_all = lax.all_gather(left_edge, 'col', axis=1, tiled=True)  10.4 us
    ppermute x8, waiting for transfers between devices, hold_the_shapes(): v1 = jax.lax.ppermute(v1, net_axis, sides)  10.4 us
    dot_general x32, matrix products, attend_row(): jnp.einsum('hjk,khd->jhd', weights, values_row, preferred_element_type=jn...  7.63 us
    dot_general x32, matrix products, attend_row(): jnp.einsum('jhd,khd->hjk', query_row, keys_row, preferred_element_type=jn...  7.44 us
  transfers between devices with their start and end apart: 19, of which 11 were waited for; matrix products, arithmetic and copies ran while one was open for 24% of the time, Pallas kernels for 0%

profile of v1, /device:TPU:0, one launch (start us, length us, event | category | flops | bytes accessed | tf_op | source)
XLA Modules:
  0.0 193.9 jit_solution(4423174295901621711)
XLA Ops:
  7.5 1.3 copy.50
  11.0 1.2 broadcast_in_dim.48
  13.4 4.9 %collective-permute-start.1 = (bf16[16,16,128]{2,1,0:T(8,128)(2,1)S(1)}, bf16[16,16,128]{2,1,0:T(8,128)(2,1)S(1)}, u32[]{:S(2)}, u32[]{:S(2)}) collective-permute-start(bf16[16,16,128]{2,1,0:T(8,128)(2,1)S(1)} %get-tuple-element.162), channel_id=1, source_target_pairs={{0,30},{2,0},{4,2},{6,4},{8,6},{10,8},{12,10},{14,12},{16,14},{18,... | collective-permute-start | bytes 196616 | tf_op jit(solution)/shard_map/ppermute | solution.py:30
  18.7 1.7 collective-permute-done
  20.4 4.4 %collective-permute-start.3 = (bf16[16,16,128]{2,1,0:T(8,128)(2,1)S(1)}, bf16[16,16,128]{2,1,0:T(8,128)(2,1)S(1)}, u32[]{:S(2)}, u32[]{:S(2)}) collective-permute-start(bf16[16,16,128]{2,1,0:T(8,128)(2,1)S(1)} %collective-permute-done.1), channel_id=1, source_target_pairs={{0,30},{2,0},{4,2},{6,4},{8,6},{10,8},{12,10},{14,12},{16,14},{18,... | collective-permute-start | bytes 196616 | tf_op jit(solution)/shard_map/ppermute | solution.py:30
  26.8 4.4 %collective-permute-start.5 = (bf16[16,16,128]{2,1,0:T(8,128)(2,1)S(1)}, bf16[16,16,128]{2,1,0:T(8,128)(2,1)S(1)}, u32[]{:S(2)}, u32[]{:S(2)}) collective-permute-start(bf16[16,16,128]{2,1,0:T(8,128)(2,1)S(1)} %collective-permute-done.3), channel_id=1, source_target_pairs={{0,30},{2,0},{4,2},{6,4},{8,6},{10,8},{12,10},{14,12},{16,14},{18,... | collective-permute-start | bytes 196616 | tf_op jit(solution)/shard_map/ppermute | solution.py:30
  33.2 4.5 %collective-permute-start.7 = (bf16[16,16,128]{2,1,0:T(8,128)(2,1)S(1)}, bf16[16,16,128]{2,1,0:T(8,128)(2,1)S(1)}, u32[]{:S(2)}, u32[]{:S(2)}) collective-permute-start(bf16[16,16,128]{2,1,0:T(8,128)(2,1)S(1)} %collective-permute-done.5), channel_id=1, source_target_pairs={{0,30},{2,0},{4,2},{6,4},{8,6},{10,8},{12,10},{14,12},{16,14},{18,... | collective-permute-start | bytes 196616 | tf_op jit(solution)/shard_map/ppermute | solution.py:30
  39.6 4.6 %collective-permute-start.9 = (bf16[16,16,128]{2,1,0:T(8,128)(2,1)S(1)}, bf16[16,16,128]{2,1,0:T(8,128)(2,1)S(1)}, u32[]{:S(2)}, u32[]{:S(2)}) collective-permute-start(bf16[16,16,128]{2,1,0:T(8,128)(2,1)S(1)} %collective-permute-done.7), channel_id=1, source_target_pairs={{0,30},{2,0},{4,2},{6,4},{8,6},{10,8},{12,10},{14,12},{16,14},{18,... | collective-permute-start | bytes 196616 | tf_op jit(solution)/shard_map/ppermute | solution.py:30
  46.1 4.6 %collective-permute-start.11 = (bf16[16,16,128]{2,1,0:T(8,128)(2,1)S(1)}, bf16[16,16,128]{2,1,0:T(8,128)(2,1)S(1)}, u32[]{:S(2)}, u32[]{:S(2)}) collective-permute-start(bf16[16,16,128]{2,1,0:T(8,128)(2,1)S(1)} %collective-permute-done.9), channel_id=1, source_target_pairs={{0,30},{2,0},{4,2},{6,4},{8,6},{10,8},{12,10},{14,12},{16,14},{18,... | collective-permute-start | bytes 196616 | tf_op jit(solution)/shard_map/ppermute | solution.py:30
  52.6 4.6 %collective-permute-start.13 = (bf16[16,16,128]{2,1,0:T(8,128)(2,1)S(1)}, bf16[16,16,128]{2,1,0:T(8,128)(2,1)S(1)}, u32[]{:S(2)}, u32[]{:S(2)}) collective-permute-start(bf16[16,16,128]{2,1,0:T(8,128)(2,1)S(1)} %collective-permute-done.11), channel_id=1, source_target_pairs={{0,30},{2,0},{4,2},{6,4},{8,6},{10,8},{12,10},{14,12},{16,14},{18,... | collective-permute-start | bytes 196616 | tf_op jit(solution)/shard_map/ppermute | solution.py:30
  60.1 5.1 %collective-permute-done.14 = bf16[16,16,128]{2,1,0:T(8,128)(2,1)S(1)} collective-permute-done((bf16[16,16,128]{2,1,0:T(8,128)(2,1)S(1)}, bf16[16,16,128]{2,1,0:T(8,128)(2,1)S(1)}, u32[]{:S(2)}, u32[]{:S(2)}) %collective-permute-start.14) | collective-permute-done | bytes 65568 | tf_op jit(solution)/shard_map/ppermute | solution.py:25
  65.9 3.6 %all-to-all-start = ((bf16[256,16,128]{2,1,0:T(8,128)(2,1)}), bf16[256,16,128]{2,1,0:T(8,128)(2,1)S(1)}, u32[]{:S(2)}, u32[]{:S(2)}) async-start(bf16[256,16,128]{2,1,0:T(8,128)(2,1)} %constant_dynamic-update-slice_fusion), calls=%async_computation | async-start | bytes 2097152 | tf_op jit(solution)/shard_map/all_to_all | solution.py:95
  69.5 10.4 %all_gather.12 = bf16[16,32,128]{2,1,0:T(8,128)(2,1)S(1)} all-gather(bf16[16,16,128]{2,1,0:T(8,128)(2,1)S(1)} %fusion.70), channel_id=1, replica_groups=mesh['row'=16,'col'=2] {'col'}, dimensions={1}, use_global_device_ids=true | all-gather | bytes 196608 | tf_op jit(solution)/shard_map/all_gather | solution.py:96
  80.9 1.4 fusion.45
  82.4 1.5 copy.54
  87.0 1.2 convolution_convert_fusion.2
  89.2 19.2 %all_gather.14 = bf16[4,256,128]{2,0,1:T(4,128)(2,1)} all-gather(bf16[4,16,128]{2,0,1:T(4,128)(2,1)S(1)} %fusion.53), channel_id=1, replica_groups=mesh['row'=16,'col'=2] {'row'}, dimensions={1}, use_global_device_ids=true | all-gather | bytes 278528 | tf_op jit(solution)/shard_map/all_gather | solution.py:114
  108.4 3.4 %all-to-all-start.1 = ((bf16[4,256,128]{2,0,1:T(4,128)(2,1)}), bf16[4,256,128]{2,0,1:T(4,128)(2,1)S(1)}, u32[]{:S(2)}, u32[]{:S(2)}) async-start(bf16[4,256,128]{2,0,1:T(4,128)(2,1)} %all_gather.14), calls=%async_computation.1 | async-start | bytes 524288 | tf_op jit(solution)/shard_map/all_to_all | solution.py:115
  111.9 1.2 convolution_convert_fusion.1
  113.5 4.2 %all-to-all-done.1 = bf16[4,256,128]{2,0,1:T(4,128)(2,1)S(1)} async-done(((bf16[4,256,128]{2,0,1:T(4,128)(2,1)}), bf16[4,256,128]{2,0,1:T(4,128)(2,1)S(1)}, u32[]{:S(2)}, u32[]{:S(2)}) %all-to-all-start.1) | async-done | bytes 262176 | tf_op jit(solution)/shard_map/all_to_all | solution.py:115
  118.5 33.0 %while.22 = (s32[]{:T(128)}, f32[16,128,2,32]{1,3,2,0:T(8,128)S(1)}, bf16[16,256,128]{2,1,0:T(8,128)(2,1)}, bf16[16,128,2,32]{1,3,2,0:T(8,128)(2,1)S(1)}, bf16[2...) while((s32[]{:T(128)}, f32[16,128,2,32]{1,3,2,0:T(8,128)S(1)}, ...), condition=%wide.region_9.10_spmd.clone, body=%wide.region_6.9_spmd.clone.sunk | while | flops 13510144 | bytes 1613165 | solution.py:67
  120.6 0.9 constant_dynamic-slice_fusion.4
  122.7 0.9 constant_dynamic-slice_fusion.4
  124.7 0.9 constant_dynamic-slice_fusion.4
  126.8 0.9 constant_dynamic-slice_fusion.4
  128.9 0.9 constant_dynamic-slice_fusion.4
  130.9 0.9 constant_dynamic-slice_fusion.4
  133.0 0.9 constant_dynamic-slice_fusion.4
  135.0 0.9 constant_dynamic-slice_fusion.4
  137.1 0.9 constant_dynamic-slice_fusion.4
  139.2 0.9 constant_dynamic-slice_fusion.4
  141.2 0.9 constant_dynamic-slice_fusion.4
  143.3 0.9 constant_dynamic-slice_fusion.4
  145.3 0.9 constant_dynamic-slice_fusion.4
  147.4 0.9 constant_dynamic-slice_fusion.4
  149.4 0.9 constant_dynamic-slice_fusion.4
  151.6 32.9 %while.23 = (s32[]{:T(128)}, f32[16,128,2,32]{1,3,2,0:T(8,128)S(1)}, bf16[16,256,128]{2,1,0:T(8,128)(2,1)}, bf16[16,128,2,32]{1,3,2,0:T(8,128)(2,1)S(1)}, bf16[2...) while((s32[]{:T(128)}, f32[16,128,2,32]{1,3,2,0:T(8,128)S(1)}, ...), condition=%wide.region_13.14_spmd.clone, body=%wide.region_10.13_spmd.clone.sunk | while | flops 13510144 | bytes 1613165 | solution.py:67
  153.6 0.9 constant_dynamic-slice_fusion.5
  155.7 0.9 constant_dynamic-slice_fusion.5
  157.8 0.9 constant_dynamic-slice_fusion.5
  159.8 0.9 constant_dynamic-slice_fusion.5
  161.9 0.9 constant_dynamic-slice_fusion.5
  163.9 0.9 constant_dynamic-slice_fusion.5
  166.0 0.9 constant_dynamic-slice_fusion.5
  168.1 0.9 constant_dynamic-slice_fusion.5
  170.1 0.9 constant_dynamic-slice_fusion.5
  172.2 0.9 constant_dynamic-slice_fusion.5
  186.0 1.0 copy.71
  (362 shorter events, 69.0 us)
Async XLA Ops:
  6.5 78.7 %copy-start = (bf16[128,128]{1,0:T(8,128)(2,1)S(1)}, bf16[128,128]{1,0:T(8,128)(2,1)}, u32[]{:S(2)}) copy-start(bf16[128,128]{1,0:T(8,128)(2,1)} %param.19) | copy-start | bytes 98308
  6.5 0.7 copy-start.4
  9.1 0.7 copy-start.5
  9.8 0.9 copy-start.3
  12.9 7.5 %collective-permute-start = (bf16[16,16,128]{2,1,0:T(8,128)(2,1)S(1)}, bf16[16,16,128]{2,1,0:T(8,128)(2,1)S(1)}, u32[]{:S(2)}, u32[]{:S(2)}) collective-permute-start(bf16[16,16,128]{2,1,0:T(8,128)(2,1)S(1)} %get-tuple-element.162), channel_id=1, source_target_pairs={{0,2},{2,4},{4,6},{6,8},{8,10},{10,12},{12,14},{14,16},{16,18},{18... | collective-permute-start | bytes 196616 | tf_op jit(solution)/shard_map/ppermute | solution.py:25
  13.4 7.0 %collective-permute-start.1 = (bf16[16,16,128]{2,1,0:T(8,128)(2,1)S(1)}, bf16[16,16,128]{2,1,0:T(8,128)(2,1)S(1)}, u32[]{:S(2)}, u32[]{:S(2)}) collective-permute-start(bf16[16,16,128]{2,1,0:T(8,128)(2,1)S(1)} %get-tuple-element.162), channel_id=1, source_target_pairs={{0,30},{2,0},{4,2},{6,4},{8,6},{10,8},{12,10},{14,12},{16,14},{18,... | collective-permute-start | bytes 196616 | tf_op jit(solution)/shard_map/ppermute | solution.py:30
  20.4 6.4 %collective-permute-start.2 = (bf16[16,16,128]{2,1,0:T(8,128)(2,1)S(1)}, bf16[16,16,128]{2,1,0:T(8,128)(2,1)S(1)}, u32[]{:S(2)}, u32[]{:S(2)}) collective-permute-start(bf16[16,16,128]{2,1,0:T(8,128)(2,1)S(1)} %collective-permute-done), channel_id=1, source_target_pairs={{0,2},{2,4},{4,6},{6,8},{8,10},{10,12},{12,14},{14,16},{16,18},{18... | collective-permute-start | bytes 196616 | tf_op jit(solution)/shard_map/ppermute | solution.py:25
  20.4 6.4 %collective-permute-start.3 = (bf16[16,16,128]{2,1,0:T(8,128)(2,1)S(1)}, bf16[16,16,128]{2,1,0:T(8,128)(2,1)S(1)}, u32[]{:S(2)}, u32[]{:S(2)}) collective-permute-start(bf16[16,16,128]{2,1,0:T(8,128)(2,1)S(1)} %collective-permute-done.1), channel_id=1, source_target_pairs={{0,30},{2,0},{4,2},{6,4},{8,6},{10,8},{12,10},{14,12},{16,14},{18,... | collective-permute-start | bytes 196616 | tf_op jit(solution)/shard_map/ppermute | solution.py:30
  26.8 6.4 %collective-permute-start.4 = (bf16[16,16,128]{2,1,0:T(8,128)(2,1)S(1)}, bf16[16,16,128]{2,1,0:T(8,128)(2,1)S(1)}, u32[]{:S(2)}, u32[]{:S(2)}) collective-permute-start(bf16[16,16,128]{2,1,0:T(8,128)(2,1)S(1)} %collective-permute-done.2), channel_id=1, source_target_pairs={{0,2},{2,4},{4,6},{6,8},{8,10},{10,12},{12,14},{14,16},{16,18},{18... | collective-permute-start | bytes 196616 | tf_op jit(solution)/shard_map/ppermute | solution.py:25
  26.8 6.4 %collective-permute-start.5 = (bf16[16,16,128]{2,1,0:T(8,128)(2,1)S(1)}, bf16[16,16,128]{2,1,0:T(8,128)(2,1)S(1)}, u32[]{:S(2)}, u32[]{:S(2)}) collective-permute-start(bf16[16,16,128]{2,1,0:T(8,128)(2,1)S(1)} %collective-permute-done.3), channel_id=1, source_target_pairs={{0,30},{2,0},{4,2},{6,4},{8,6},{10,8},{12,10},{14,12},{16,14},{18,... | collective-permute-start | bytes 196616 | tf_op jit(solution)/shard_map/ppermute | solution.py:30
  33.2 6.4 %collective-permute-start.6 = (bf16[16,16,128]{2,1,0:T(8,128)(2,1)S(1)}, bf16[16,16,128]{2,1,0:T(8,128)(2,1)S(1)}, u32[]{:S(2)}, u32[]{:S(2)}) collective-permute-start(bf16[16,16,128]{2,1,0:T(8,128)(2,1)S(1)} %collective-permute-done.4), channel_id=1, source_target_pairs={{0,2},{2,4},{4,6},{6,8},{8,10},{10,12},{12,14},{14,16},{16,18},{18... | collective-permute-start | bytes 196616 | tf_op jit(solution)/shard_map/ppermute | solution.py:25
  33.2 6.4 %collective-permute-start.7 = (bf16[16,16,128]{2,1,0:T(8,128)(2,1)S(1)}, bf16[16,16,128]{2,1,0:T(8,128)(2,1)S(1)}, u32[]{:S(2)}, u32[]{:S(2)}) collective-permute-start(bf16[16,16,128]{2,1,0:T(8,128)(2,1)S(1)} %collective-permute-done.5), channel_id=1, source_target_pairs={{0,30},{2,0},{4,2},{6,4},{8,6},{10,8},{12,10},{14,12},{16,14},{18,... | collective-permute-start | bytes 196616 | tf_op jit(solution)/shard_map/ppermute | solution.py:30
  39.6 6.4 %collective-permute-start.8 = (bf16[16,16,128]{2,1,0:T(8,128)(2,1)S(1)}, bf16[16,16,128]{2,1,0:T(8,128)(2,1)S(1)}, u32[]{:S(2)}, u32[]{:S(2)}) collective-permute-start(bf16[16,16,128]{2,1,0:T(8,128)(2,1)S(1)} %collective-permute-done.6), channel_id=1, source_target_pairs={{0,2},{2,4},{4,6},{6,8},{8,10},{10,12},{12,14},{14,16},{16,18},{18... | collective-permute-start | bytes 196616 | tf_op jit(solution)/shard_map/ppermute | solution.py:25
  39.6 6.5 %collective-permute-start.9 = (bf16[16,16,128]{2,1,0:T(8,128)(2,1)S(1)}, bf16[16,16,128]{2,1,0:T(8,128)(2,1)S(1)}, u32[]{:S(2)}, u32[]{:S(2)}) collective-permute-start(bf16[16,16,128]{2,1,0:T(8,128)(2,1)S(1)} %collective-permute-done.7), channel_id=1, source_target_pairs={{0,30},{2,0},{4,2},{6,4},{8,6},{10,8},{12,10},{14,12},{16,14},{18,... | collective-permute-start | bytes 196616 | tf_op jit(solution)/shard_map/ppermute | solution.py:30
  46.0 6.5 %collective-permute-start.10 = (bf16[16,16,128]{2,1,0:T(8,128)(2,1)S(1)}, bf16[16,16,128]{2,1,0:T(8,128)(2,1)S(1)}, u32[]{:S(2)}, u32[]{:S(2)}) collective-permute-start(bf16[16,16,128]{2,1,0:T(8,128)(2,1)S(1)} %collective-permute-done.8), channel_id=1, source_target_pairs={{0,2},{2,4},{4,6},{6,8},{8,10},{10,12},{12,14},{14,16},{16,18},{18... | collective-permute-start | bytes 196616 | tf_op jit(solution)/shard_map/ppermute | solution.py:25
  46.1 6.5 %collective-permute-start.11 = (bf16[16,16,128]{2,1,0:T(8,128)(2,1)S(1)}, bf16[16,16,128]{2,1,0:T(8,128)(2,1)S(1)}, u32[]{:S(2)}, u32[]{:S(2)}) collective-permute-start(bf16[16,16,128]{2,1,0:T(8,128)(2,1)S(1)} %collective-permute-done.9), channel_id=1, source_target_pairs={{0,30},{2,0},{4,2},{6,4},{8,6},{10,8},{12,10},{14,12},{16,14},{18,... | collective-permute-start | bytes 196616 | tf_op jit(solution)/shard_map/ppermute | solution.py:30
  52.5 6.4 %collective-permute-start.12 = (bf16[16,16,128]{2,1,0:T(8,128)(2,1)S(1)}, bf16[16,16,128]{2,1,0:T(8,128)(2,1)S(1)}, u32[]{:S(2)}, u32[]{:S(2)}) collective-permute-start(bf16[16,16,128]{2,1,0:T(8,128)(2,1)S(1)} %collective-permute-done.10), channel_id=1, source_target_pairs={{0,2},{2,4},{4,6},{6,8},{8,10},{10,12},{12,14},{14,16},{16,18},{18... | collective-permute-start | bytes 196616 | tf_op jit(solution)/shard_map/ppermute | solution.py:25
  52.6 6.9 %collective-permute-start.13 = (bf16[16,16,128]{2,1,0:T(8,128)(2,1)S(1)}, bf16[16,16,128]{2,1,0:T(8,128)(2,1)S(1)}, u32[]{:S(2)}, u32[]{:S(2)}) collective-permute-start(bf16[16,16,128]{2,1,0:T(8,128)(2,1)S(1)} %collective-permute-done.11), channel_id=1, source_target_pairs={{0,30},{2,0},{4,2},{6,4},{8,6},{10,8},{12,10},{14,12},{16,14},{18,... | collective-permute-start | bytes 196616 | tf_op jit(solution)/shard_map/ppermute | solution.py:30
  58.9 6.4 %collective-permute-start.14 = (bf16[16,16,128]{2,1,0:T(8,128)(2,1)S(1)}, bf16[16,16,128]{2,1,0:T(8,128)(2,1)S(1)}, u32[]{:S(2)}, u32[]{:S(2)}) collective-permute-start(bf16[16,16,128]{2,1,0:T(8,128)(2,1)S(1)} %collective-permute-done.12), channel_id=1, source_target_pairs={{0,2},{2,4},{4,6},{6,8},{8,10},{10,12},{12,14},{14,16},{16,18},{18... | collective-permute-start | bytes 196616 | tf_op jit(solution)/shard_map/ppermute | solution.py:25
  65.9 16.5 %all-to-all-start = ((bf16[256,16,128]{2,1,0:T(8,128)(2,1)}), bf16[256,16,128]{2,1,0:T(8,128)(2,1)S(1)}, u32[]{:S(2)}, u32[]{:S(2)}) async-start(bf16[256,16,128]{2,1,0:T(8,128)(2,1)} %constant_dynamic-update-slice_fusion), calls=%async_computation | async-start | bytes 2097152 | tf_op jit(solution)/shard_map/all_to_all | solution.py:95
  69.5 49.0 %all-gather.3.cloned.1.call-start = ((), (), s32[]{:S(2)}) async-start(), calls=%async_computation.2 | async-start | bytes 1572864 | tf_op jit(solution)/shard_map/all_gather | solution.py:131
  79.9 0.9 copy-start.2
  84.3 0.7 copy-start.6
  84.5 1.2 copy-start.1
  86.3 0.7 copy-start.7
  88.2 0.7 copy-start.9
  108.4 9.4 %all-to-all-start.1 = ((bf16[4,256,128]{2,0,1:T(4,128)(2,1)}), bf16[4,256,128]{2,0,1:T(4,128)(2,1)S(1)}, u32[]{:S(2)}, u32[]{:S(2)}) async-start(bf16[4,256,128]{2,0,1:T(4,128)(2,1)} %all_gather.14), calls=%async_computation.1 | async-start | bytes 524288 | tf_op jit(solution)/shard_map/all_to_all | solution.py:115
  111.9 39.7 %all-gather.5.cloned.1.call-start = ((), (), s32[]{:S(2)}) async-start(), calls=%async_computation.3 | async-start | bytes 1572864 | tf_op jit(solution)/shard_map/all_gather | solution.py:131
  184.5 0.8 copy-start.8
Sparse Core Ops, SparseCore 0:
  88.3 17.2 all-gather.2
  114.2 20.4 all-gather.4
